TPU v7x, 32 devices: a whole 2x2x4 slice. The times are simulated.
32 devices in a mesh: lat: 16 (over z, y, x), ray: 2 (over core).
Axes of the slice: x: 2, y: 2, z: 4, core: 2. Of those that a mesh axis runs over, the one named last changes fastest.
Arguments:
- kernels: float32 [256, 4, 128, 128], P(('lat', 'ray')), may hold values from -0.25 to 0.25
- pattern: int32 [256, 4], P(('lat', 'ray')), may hold values from 0 to 255, as said below
- offsets: int32 [4], replicated, may hold values from 1 to 128, as said below
- smooth_weight: float32 [4, 256, 128], P(None, 'lat'), may hold values from 0.2 to 1
- u_data: float32 [256, 128], P(('lat', 'ray')), may hold values from -16 to 16
- u_smooth: float32 [4, 256, 128], P(None, 'lat'), may hold values from -6 to 6
- right_vector: float32 [256, 128], P('lat'), may hold values from -16 to 16
- direction: float32 [256, 128], P('lat'), may hold values from -6 to 6
- model_estimate: float32 [256, 128], P('lat'), may hold values from -6 to 6
- recurrence: float32 [3], replicated, may hold values from 0.5 to 2
Outputs:
- u_data_new: float32 [256, 128], P(('lat', 'ray'))
- u_smooth_new: float32 [4, 256, 128], P(None, 'lat')
- v_new: float32 [256, 128], P('lat')
- w_new: float32 [256, 128], P('lat')
- x_new: float32 [256, 128], P('lat')
- scalars: float32 [4], replicated
Inputs may be any that keep to these rules, and one draw needn't show every extreme that they name: `pattern`: in each aligned block of 8 ray blocks (the rows of one device), the tiles of any one longitude band are named by exactly 2 kernel blocks or by none; kernel blocks of the same rows that name the same band name different tiles; the 4 tiles of a ray block differ. `offsets`: the last offset is 128.
All inputs are finite; a program needn't handle non-finite values.
Results may differ from a plain program's by a relative error of at most 0.00007.
Values sent between devices are 32-bit elements; how exact they have to be, the bound alone decides.
A program may use at most 64 MiB of HBM per device.

v0:
```python
import jax
import jax.numpy as jnp
from jax import lax
from jax.sharding import PartitionSpec as P

EPS = 1e-06


def from_behind(value, axis, steps):
    count = lax.axis_size(axis)
    pairs = [(source, (source + steps) % count) for source in range(count)]
    return lax.ppermute(value, axis, pairs)


def local(
    kernels,
    pattern,
    offsets,
    smooth_weight,
    u_data,
    u_smooth,
    right_vector,
    direction,
    model_estimate,
    recurrence,
):
    highest = lax.Precision.HIGHEST
    alpha_old = recurrence[0]
    rhobar_old = recurrence[1]
    phibar_old = recurrence[2]
    stencil = offsets.shape[0]
    tiles_dev = right_vector.shape[0]
    block = right_vector.shape[1]
    blocks_dev = pattern.shape[0]
    kernel_count = pattern.shape[1]
    band = tiles_dev * block
    lat_count = lax.axis_size("lat")
    ray_count = lax.axis_size("ray")
    cell_count = band * lat_count
    rows_all = blocks_dev * lat_count * ray_count * block + stencil * cell_count
    ratio = cell_count / rows_all
    own = right_vector.reshape(-1)
    slot_total = blocks_dev * kernel_count
    capacity = max(2, -(-slot_total // lat_count))
    flat_pattern = pattern.reshape(-1)
    owner_band = flat_pattern // tiles_dev
    local_tile = flat_pattern % tiles_dev
    slot_order = jnp.arange(slot_total, dtype=jnp.int32)
    earlier = (owner_band[:, None] == owner_band[None, :]) & (
        slot_order[None, :] < slot_order[:, None]
    )
    slot_rank = jnp.sum(earlier.astype(jnp.int32), axis=1)
    requests = jnp.zeros((lat_count, capacity), jnp.int32).at[owner_band, slot_rank].set(local_tile)
    asked = lax.all_to_all(requests, "lat", split_axis=0, concat_axis=0, tiled=True)
    tiles_out = right_vector[asked]
    returned = lax.all_to_all(tiles_out, "lat", split_axis=0, concat_axis=0, tiled=True)
    picked = returned[owner_band, slot_rank].reshape(blocks_dev, kernel_count, block)
    east = from_behind(right_vector[:1], "lat", -1)
    data_raw = jnp.einsum("bkij,bkj->bi", kernels, picked, precision=highest) - alpha_old * u_data
    window = jnp.concatenate([own, east.reshape(-1)])
    ahead = jnp.stack([lax.dynamic_slice_in_dim(window, offsets[s], band) for s in range(stencil)])
    smooth_raw = (
        smooth_weight * (own[None, :] - ahead).reshape(stencil, tiles_dev, block)
        - alpha_old * u_smooth
    )
    local_rows = jnp.sum(data_raw * data_raw) + jnp.sum(smooth_raw * smooth_raw) / ray_count
    contrib = jnp.einsum("bkij,bi->bkj", kernels, data_raw, precision=highest)
    weighted = (smooth_weight * smooth_raw).reshape(stencil, band)
    rim = from_behind(weighted[:, band - block :], "lat", 1)
    padded = jnp.concatenate([rim, weighted], axis=1)
    behind = jnp.stack(
        [lax.dynamic_slice_in_dim(padded[s], block - offsets[s], band) for s in range(stencil)]
    )
    smooth_adj = jnp.sum(weighted - behind, axis=0)
    beta = jnp.sqrt(lax.psum(local_rows, ("lat", "ray")) / rows_all + EPS)
    outgoing = (
        jnp.zeros((lat_count, capacity, block), jnp.float32)
        .at[owner_band, slot_rank]
        .set(contrib.reshape(slot_total, block))
    )
    incoming = lax.all_to_all(outgoing, "lat", split_axis=0, concat_axis=0, tiled=True)
    selector = (
        asked.reshape(-1)[:, None] == jnp.arange(tiles_dev, dtype=jnp.int32)[None, :]
    ).astype(jnp.float32)
    partial_band = jnp.einsum("st,sj->tj", selector, incoming.reshape(-1, block), precision=highest)
    summed = lax.psum(partial_band, "ray").reshape(-1) + smooth_adj
    v_raw = ratio * summed / beta - beta * own
    model_sq = lax.psum(jnp.sum(v_raw * v_raw) / ray_count, ("lat", "ray"))
    alpha = jnp.sqrt(model_sq / cell_count + EPS)
    v_piece = v_raw / alpha
    v_new = v_piece.reshape(tiles_dev, block)
    rho = jnp.sqrt(rhobar_old * rhobar_old + beta * beta)
    cosine = rhobar_old / rho
    sine = beta / rho
    theta = sine * alpha
    rhobar = -cosine * alpha
    phi = cosine * phibar_old
    phibar = sine * phibar_old
    x_new = model_estimate + phi / rho * direction
    w_new = v_new - theta / rho * direction
    scalars = jnp.stack([alpha, beta, rhobar, phibar])
    return (data_raw / beta, smooth_raw / beta, v_new, w_new, x_new, scalars)


def solution(mesh):
    return jax.shard_map(
        local,
        mesh=mesh,
        in_specs=(
            P(("lat", "ray"), None, None, None),
            P(("lat", "ray"), None),
            P(),
            P(None, "lat", None),
            P(("lat", "ray"), None),
            P(None, "lat", None),
            P("lat", None),
            P("lat", None),
            P("lat", None),
            P(),
        ),
        out_specs=(
            P(("lat", "ray"), None),
            P(None, "lat", None),
            P("lat", None),
            P("lat", None),
            P("lat", None),
            P(),
        ),
        check_vma=False,
    )
```

profile of v0, /device:TPU:0, one launch (start us, length us, event | category | flops | bytes accessed | tf_op | source)
XLA Modules:
  0.0 158.8 jit_solution(6131606024387064585)
XLA Ops:
  0.6 0.8 slice.44
  1.5 7.0 %collective-permute-start = (f32[1,128]{1,0:T(1,128)S(1)}, f32[1,128]{1,0:T(1,128)S(1)}, u32[]{:S(2)}, u32[]{:S(2)}) collective-permute-start(f32[1,128]{1,0:T(1,128)S(1)} %slice.44), channel_id=1, source_target_pairs={{0,30},{2,0},{4,2},{6,4},{8,6},{10,8},{12,10},{14,12},{16,14},{18,... | collective-permute-start | bytes 1544 | tf_op jit(solution)/shard_map/ppermute | solution.py:12
  8.4 0.8 copy.29
  9.6 2.0 %scatter_fusion = s32[16,2]{0,1:T(2,128)S(1)} fusion(s32[16,2]{0,1:T(2,128)S(1)} %broadcast.162, s32[32]{0:T(128)S(1)} %fusion.15, s32[32]{0:T(128)S(1)} %get-tuple-element.32), kind=kCustom, calls=%fused_computation.2 | custom fusion | bytes 640 | tf_op jit(solution)/shard_map/scatter | solution.py:53
  11.7 0.7 copy.31
  12.3 3.5 %all-to-all-start = ((s32[16,1,2]{2,1,0:T(1,128)}), s32[16,1,2]{2,1,0:T(1,128)S(1)}, u32[]{:S(2)}, u32[]{:S(2)}) async-start(s32[16,1,2]{2,1,0:T(1,128)} %copy.31), calls=%async_computation | async-start | bytes 16384 | tf_op jit(solution)/shard_map/all_to_all | solution.py:54
  15.8 1.5 fusion.21
  27.5 1.4 fusion.20
  33.0 1.9 %gather_fusion = f32[32,128]{1,0:T(8,128)} fusion(f32[16,128]{1,0:T(8,128)} %param.16, s32[1024]{0:T(1024)S(1)} %pad_clamp_fusion), kind=kCustom, calls=%fused_computation | custom fusion | bytes 32896 | tf_op jit(solution)/shard_map/gather | solution.py:55
  34.8 6.9 %all-to-all-start.1 = ((f32[16,2,128]{2,1,0:T(2,128)}), f32[16,2,128]{2,1,0:T(2,128)S(1)}, u32[]{:S(2)}, u32[]{:S(2)}) async-start(f32[16,2,128]{2,1,0:T(2,128)} %bitcast.4), calls=%async_computation.1 | async-start | bytes 32768 | tf_op jit(solution)/shard_map/all_to_all | solution.py:56
  43.0 1.0 fusion.8
  44.0 1.4 fusion.17
  45.4 2.0 %collective-permute-start.1 = (f32[4,128]{1,0:T(4,128)S(1)}, f32[4,128]{1,0:T(4,128)S(1)}, u32[]{:S(2)}, u32[]{:S(2)}) collective-permute-start(f32[4,128]{1,0:T(4,128)S(1)} %slice.64), channel_id=1, source_target_pairs={{0,2},{2,4},{4,6},{6,8},{8,10},{10,12},{12,14},{14,16},{16,18},{18... | collective-permute-start | bytes 6152 | tf_op jit(solution)/shard_map/ppermute | solution.py:12
  48.7 4.0 %collective-permute-done.1 = f32[4,128]{1,0:T(4,128)S(1)} collective-permute-done((f32[4,128]{1,0:T(4,128)S(1)}, f32[4,128]{1,0:T(4,128)S(1)}, u32[]{:S(2)}, u32[]{:S(2)}) %collective-permute-start.1) | collective-permute-done | bytes 2080 | tf_op jit(solution)/shard_map/ppermute | solution.py:12
  53.0 0.7 gather_fusion.1
  53.7 1.8 %fusion.22 = f32[8,1,128,1]{2,1,3,0:T(1,128)S(1)} fusion(f32[8,4,128,1]{2,3,1,0:T(1,128)S(1)} %bitcast.77, f32[8,4,128,128]{3,2,1,0:T(8,128)S(1)} %copy-done), kind=kOutput, calls=%fused_computation.72 | convolution fusion | flops 6291456 | bytes 2117632 | tf_op jit(solution)/shard_map/bkij,bkj->bi/dot_general | solution.py:59
  55.5 1.3 multiply_reduce_fusion.2
  57.4 37.9 %psum.21 = f32[]{:T(128)} all-reduce(f32[]{:T(128)S(6)} %add.121), channel_id=1, replica_groups=mesh['lat'=16,'ray'=2] {'lat','ray'}, use_global_device_ids=true, to_apply=%region_4.5 | all-reduce | flops 1 | bytes 8 | tf_op jit(solution)/shard_map/psum | solution.py:75
  96.0 1.1 fusion.23
  97.7 3.8 %scatter_fusion.1 = f32[16,2,128]{2,1,0:T(2,128)} fusion(f32[16,2,128]{2,1,0:T(2,128)} %broadcast_in_dim.2, s32[32]{0:T(128)S(1)} %fusion.15, f32[32,128]{1,0:T(8,128)S(1)} %bitcast.76), kind=kCustom, calls=%fused_computation.3 | custom fusion | bytes 49408 | tf_op jit(solution)/shard_map/scatter | solution.py:79
  101.5 5.7 %all-to-all-start.2 = ((f32[16,2,128]{2,1,0:T(2,128)}), f32[16,2,128]{2,1,0:T(2,128)S(1)}, u32[]{:S(2)}, u32[]{:S(2)}) async-start(f32[16,2,128]{2,1,0:T(2,128)} %scatter_fusion.1), calls=%async_computation.2 | async-start | bytes 32768 | tf_op jit(solution)/shard_map/all_to_all | solution.py:81
  110.5 4.1 %all-to-all-done.2 = f32[16,2,128]{2,1,0:T(2,128)S(1)} async-done(((f32[16,2,128]{2,1,0:T(2,128)}), f32[16,2,128]{2,1,0:T(2,128)S(1)}, u32[]{:S(2)}, u32[]{:S(2)}) %all-to-all-start.2) | async-done | bytes 16416 | tf_op jit(solution)/shard_map/all_to_all | solution.py:81
  114.8 2.5 %psum.22 = f32[16,128]{1,0:T(8,128)S(1)} all-reduce(f32[16,128]{1,0:T(8,128)S(1)} %fusion.4), channel_id=1, replica_groups=mesh['lat'=16,'ray'=2] {'ray'}, use_global_device_ids=true, to_apply=%region_6.7 | all-reduce | flops 2048 | bytes 16384 | tf_op jit(solution)/shard_map/psum | solution.py:86
  118.6 38.3 %psum.23 = f32[]{:T(128)} all-reduce(f32[]{:T(128)S(6)} %div.87), channel_id=1, replica_groups=mesh['lat'=16,'ray'=2] {'lat','ray'}, use_global_device_ids=true, to_apply=%region_9.10 | all-reduce | flops 1 | bytes 8 | tf_op jit(solution)/shard_map/psum | solution.py:88
  (44 shorter events, 6.7 us)
Async XLA Ops:
  0.6 53.0 %copy-start = (f32[8,4,128,128]{3,2,1,0:T(8,128)S(1)}, f32[8,4,128,128]{3,2,1,0:T(8,128)}, u32[]{:S(2)}) copy-start(f32[8,4,128,128]{3,2,1,0:T(8,128)} %param.10) | copy-start | bytes 6291460
  1.5 41.5 %collective-permute-start = (f32[1,128]{1,0:T(1,128)S(1)}, f32[1,128]{1,0:T(1,128)S(1)}, u32[]{:S(2)}, u32[]{:S(2)}) collective-permute-start(f32[1,128]{1,0:T(1,128)S(1)} %slice.44), channel_id=1, source_target_pairs={{0,30},{2,0},{4,2},{6,4},{8,6},{10,8},{12,10},{14,12},{16,14},{18,... | collective-permute-start | bytes 1544 | tf_op jit(solution)/shard_map/ppermute | solution.py:12
  9.6 45.9 %copy-start.4 = (f32[8,128]{1,0:T(8,128)S(1)}, f32[8,128]{1,0:T(8,128)}, u32[]{:S(2)}) copy-start(f32[8,128]{1,0:T(8,128)} %param.14) | copy-start | bytes 12292
  12.3 20.3 %all-to-all-start = ((s32[16,1,2]{2,1,0:T(1,128)}), s32[16,1,2]{2,1,0:T(1,128)S(1)}, u32[]{:S(2)}, u32[]{:S(2)}) async-start(s32[16,1,2]{2,1,0:T(1,128)} %copy.31), calls=%async_computation | async-start | bytes 16384 | tf_op jit(solution)/shard_map/all_to_all | solution.py:54
  34.8 18.1 %all-to-all-start.1 = ((f32[16,2,128]{2,1,0:T(2,128)}), f32[16,2,128]{2,1,0:T(2,128)S(1)}, u32[]{:S(2)}, u32[]{:S(2)}) async-start(f32[16,2,128]{2,1,0:T(2,128)} %bitcast.4), calls=%async_computation.1 | async-start | bytes 32768 | tf_op jit(solution)/shard_map/all_to_all | solution.py:56
  45.4 7.2 %collective-permute-start.1 = (f32[4,128]{1,0:T(4,128)S(1)}, f32[4,128]{1,0:T(4,128)S(1)}, u32[]{:S(2)}, u32[]{:S(2)}) collective-permute-start(f32[4,128]{1,0:T(4,128)S(1)} %slice.64), channel_id=1, source_target_pairs={{0,2},{2,4},{4,6},{6,8},{8,10},{10,12},{12,14},{14,16},{16,18},{18... | collective-permute-start | bytes 6152 | tf_op jit(solution)/shard_map/ppermute | solution.py:12
  53.6 63.6 %copy-start.1 = (f32[16,128]{1,0:T(8,128)S(1)}, f32[16,128]{1,0:T(8,128)}, u32[]{:S(2)}) copy-start(f32[16,128]{1,0:T(8,128)} %param.16) | copy-start | bytes 24580
  53.6 104.5 %copy-start.2 = (f32[16,128]{1,0:T(8,128)S(1)}, f32[16,128]{1,0:T(8,128)}, u32[]{:S(2)}) copy-start(f32[16,128]{1,0:T(8,128)} %param.17) | copy-start | bytes 24580
  53.6 104.5 %copy-start.3 = (f32[16,128]{1,0:T(8,128)S(1)}, f32[16,128]{1,0:T(8,128)}, u32[]{:S(2)}) copy-start(f32[16,128]{1,0:T(8,128)} %param.18) | copy-start | bytes 24580
  101.5 13.0 %all-to-all-start.2 = ((f32[16,2,128]{2,1,0:T(2,128)}), f32[16,2,128]{2,1,0:T(2,128)S(1)}, u32[]{:S(2)}, u32[]{:S(2)}) async-start(f32[16,2,128]{2,1,0:T(2,128)} %scatter_fusion.1), calls=%async_computation.2 | async-start | bytes 32768 | tf_op jit(solution)/shard_map/all_to_all | solution.py:81
where the time goes:
time: 160 us; the launch traced here: 159 us
  blocking collectives  78.6 us (49%)
  starting transfers between devices  25 us (16%)
  between operations  20.4 us (13%)
  local copies, waits for them, and re-layouts  15.4 us (10%)
  other arithmetic  8.21 us (5%)
  waiting for transfers between devices  8.08 us (5%)
  matrix products  3.18 us (2%)
    psum x1, blocking collectives, local(): model_sq = lax.psum(jnp.sum(v_raw * v_raw) / ray_count, ('lat', 'ray'))  38.3 us
    psum x1, blocking collectives, local(): beta = jnp.sqrt(lax.psum(local_rows, ('lat', 'ray')) / rows_all + EPS)  37.9 us
    ppermute x2, starting transfers between devices, from_behind(): return lax.ppermute(value, axis, pairs)  8.94 us
    all_to_all x1, starting transfers between devices, local(): lax.all_to_all(tiles_out, 'lat', split_axis=0, concat_axis=0, tiled=True)  6.88 us
    all_to_all x1, starting transfers between devices, local(): lax.all_to_all(outgoing, 'lat', split_axis=0, concat_axis=0, tiled=True)  5.68 us
    all_to_all x1, waiting for transfers between devices, local(): lax.all_to_all(outgoing, 'lat', split_axis=0, concat_axis=0, tiled=True)  4.07 us
    ppermute x2, waiting for transfers between devices, from_behind(): return lax.ppermute(value, axis, pairs)  4 us
    scatter x1, local copies, waits for them, and re-layouts, local(): outgoing = jnp.zeros((lat_count, capacity, block), jnp.float32).at[owner_...  3.79 us
  transfers between devices with their start and end apart: 5, of which 2 were waited for; matrix products, arithmetic and copies ran while one was open for 9% of the time, Pallas kernels for 0%

commit v1 on v0

v1 whole, which is shorter than its diff:
```python
import functools

import jax
import jax.numpy as jnp
from jax import lax
from jax.experimental import pallas as pl
from jax.experimental.pallas import tpu as pltpu
from jax.sharding import PartitionSpec as P

EPS = 1e-06
MESH = pl.DeviceIdType.MESH
F32 = jnp.float32
HIGHEST = lax.Precision.HIGHEST
ROWS = 4
GROUP = 32


def kernel(
    n_lat,
    n_ray,
    pattern,
    offsets,
    recurrence,
    kernels_hbm,
    smooth_weight,
    u_data,
    u_smooth,
    right_vector,
    direction,
    model_estimate,
    u_data_new,
    u_smooth_new,
    v_new,
    w_new,
    x_new,
    scalars,
    held,
    full,
    window,
    padded,
    smooth_raw,
    data_raw,
    contrib,
    message,
    inbox,
    square,
    squares,
    local_sem,
    send_sem,
    recv_sem,
):
    lat = lax.axis_index("lat")
    ray = lax.axis_index("ray")
    n_dev = n_lat * n_ray
    me = lat * n_ray + ray
    blocks_dev, kernel_count, block, _ = held.shape
    tiles_dev = right_vector.shape[0]
    stencil = smooth_weight.shape[0]
    slots = blocks_dev * kernel_count
    cell_count = n_lat * tiles_dev * block
    rows_all = n_dev * blocks_dev * block + stencil * cell_count
    ratio = cell_count / rows_all

    fetch = pltpu.make_async_copy(kernels_hbm, held, local_sem.at[0])
    fetch.start()
    own_band = pltpu.make_async_copy(
        right_vector, full.at[pl.ds(lat * tiles_dev, tiles_dev)], local_sem.at[1]
    )
    own_band.start()

    barrier = pltpu.get_barrier_semaphore()

    def greet(step, carry):
        other = lax.rem(me + step, n_dev)
        pl.semaphore_signal(
            barrier,
            inc=1,
            device_id=(lax.div(other, n_ray), lax.rem(other, n_ray)),
            device_id_type=MESH,
        )
        return carry

    lax.fori_loop(1, n_dev, greet, 0)
    pl.semaphore_wait(barrier, n_dev - 1)

    def send_band(step, carry):
        pltpu.make_async_remote_copy(
            src_ref=right_vector,
            dst_ref=full.at[pl.ds(lat * tiles_dev, tiles_dev)],
            send_sem=send_sem.at[0],
            recv_sem=recv_sem.at[0],
            device_id=(lax.rem(lat + step, n_lat), ray),
            device_id_type=MESH,
        ).start()
        return carry

    lax.fori_loop(1, n_lat, send_band, 0)

    alpha_old = recurrence[0]
    lane_slot = lax.broadcasted_iota(jnp.int32, (1, slots), 1)
    tile_row = jnp.zeros((1, slots), F32)
    for b in range(blocks_dev):
        for k in range(kernel_count):
            tile_row = jnp.where(
                lane_slot == b * kernel_count + k, pattern[b, k].astype(F32), tile_row
            )
    shape = (n_lat * ROWS, slots)
    message_row = lax.broadcasted_iota(jnp.int32, shape, 0)
    slot = lax.broadcasted_iota(jnp.int32, shape, 1).astype(F32)
    kind = message_row & (ROWS - 1)
    local_tile = tile_row - ((message_row // ROWS) * tiles_dev).astype(F32)
    in_band = (local_tile >= 0) & (local_tile < tiles_dev)
    first = jnp.min(jnp.where(in_band, slot, F32(slots)), axis=1, keepdims=True)
    is_first = in_band & (slot == first)
    is_second = in_band & (slot != first)
    selector = jnp.where(
        (is_first & (kind == 0)) | (is_second & (kind == 1)), F32(1), F32(0)
    )
    first_tile = jnp.sum(jnp.where(is_first, local_tile + 1, F32(0)), axis=1, keepdims=True)
    second_tile = jnp.sum(jnp.where(is_second, local_tile + 1, F32(0)), axis=1, keepdims=True)
    wide = (n_lat * ROWS, block)
    lane_wide = lax.broadcasted_iota(jnp.int32, wide, 1)
    kind_wide = lax.broadcasted_iota(jnp.int32, wide, 0) & (ROWS - 1)
    mark = lax.rem(me, GROUP) * ROWS
    header = jnp.where(
        lane_wide == mark,
        first_tile,
        jnp.where(lane_wide == mark + 1, second_tile, F32(0)),
    )
    header = jnp.where(kind_wide == 2, header, F32(0))
    is_total = (kind_wide == 2) & (lane_wide == mark + 2)

    fetch.wait()
    own_band.wait()
    rest = pl.ds(0, (n_lat - 1) * tiles_dev)
    bands = pltpu.make_async_remote_copy(
        src_ref=full.at[rest],
        dst_ref=full.at[rest],
        send_sem=send_sem.at[0],
        recv_sem=recv_sem.at[0],
        device_id=(lat, ray),
        device_id_type=MESH,
    )
    bands.wait_recv()

    diagonal = lax.broadcasted_iota(jnp.int32, (block, block), 0) == lax.broadcasted_iota(
        jnp.int32, (block, block), 1
    )
    for b in range(blocks_dev):
        total = jnp.where(diagonal, -alpha_old * u_data[b : b + 1, :], F32(0))
        for k in range(kernel_count):
            total = total + held[b, k] * full[pl.ds(pattern[b, k], 1), :]
        column = jnp.sum(total, axis=1, keepdims=True)
        data_raw[b : b + 1, :] = jnp.sum(
            jnp.where(diagonal, column, F32(0)), axis=0, keepdims=True
        )
        for k in range(kernel_count):
            contrib[b * kernel_count + k : b * kernel_count + k + 1, :] = jnp.sum(
                held[b, k] * column, axis=0, keepdims=True
            )

    own = right_vector[...]
    lane = lax.broadcasted_iota(jnp.int32, (1, block), 1)
    window[0:tiles_dev, :] = own
    window[tiles_dev : tiles_dev + 1, :] = full[
        pl.ds(lax.rem(lat + 1, n_lat) * tiles_dev, 1), :
    ]
    below = window[1 : tiles_dev + 1, :]
    rim = jnp.zeros((1, block), F32)
    smooth_square = jnp.zeros((tiles_dev, block), F32)
    for s in range(stencil):
        offset = offsets[s]
        back = (block - offset) & (block - 1)
        ahead = jnp.where(
            lane < block - offset, pltpu.roll(own, back, 1), pltpu.roll(below, back, 1)
        )
        raw = smooth_weight[s] * (own - ahead) - alpha_old * u_smooth[s]
        smooth_raw[s] = raw
        smooth_square = smooth_square + raw * raw
        weighted = smooth_weight[s] * raw
        padded[s, 8 : 8 + tiles_dev, :] = weighted
        turned = pltpu.roll(weighted, offset & (block - 1), 1)
        rim = rim + jnp.where(lane < offset, turned[tiles_dev - 1 : tiles_dev, :], F32(0))
    raw = data_raw[...]
    row_sum = jnp.sum(raw * raw, axis=0, keepdims=True) + (
        jnp.sum(smooth_square, axis=0, keepdims=True) * (1.0 / n_ray)
    )
    local_total = jnp.sum(row_sum, axis=1, keepdims=True)

    picked = jnp.dot(selector, contrib[...], precision=HIGHEST, preferred_element_type=F32)
    outgoing = (
        picked
        + header
        + jnp.where(is_total, local_total, F32(0))
        + jnp.where(kind_wide == 3, rim, F32(0))
    )
    for band in range(n_lat):
        message[band] = outgoing[band * ROWS : (band + 1) * ROWS, :]

    def send_message(step, carry):
        other = lax.rem(me + step, n_dev)
        pltpu.make_async_remote_copy(
            src_ref=message.at[lax.div(other, n_ray)],
            dst_ref=inbox.at[me],
            send_sem=send_sem.at[1],
            recv_sem=recv_sem.at[1],
            device_id=(lax.div(other, n_ray), lax.rem(other, n_ray)),
            device_id_type=MESH,
        ).start()
        return carry

    lax.fori_loop(1, n_dev, send_message, 0)
    inbox[me] = message[lat]

    smooth_adjoint = jnp.zeros((tiles_dev, block), F32)
    for s in range(stencil):
        offset = offsets[s]
        padded[s, 7:8, :] = jnp.zeros((1, block), F32)
        weighted = padded[s, 8 : 8 + tiles_dev, :]
        above = padded[s, 7 : 7 + tiles_dev, :]
        behind = jnp.where(
            lane >= offset,
            pltpu.roll(weighted, offset & (block - 1), 1),
            pltpu.roll(above, offset & (block - 1), 1),
        )
        smooth_adjoint = smooth_adjoint + (weighted - behind)

    bands.wait_send()
    others = pl.ds(0, n_dev - 1)
    messages = pltpu.make_async_remote_copy(
        src_ref=inbox.at[others],
        dst_ref=inbox.at[others],
        send_sem=send_sem.at[1],
        recv_sem=recv_sem.at[1],
        device_id=(lat, ray),
        device_id_type=MESH,
    )
    messages.wait_recv()

    group = min(GROUP, n_dev)
    lane_group = lax.broadcasted_iota(jnp.int32, (1, group * ROWS), 1)
    tile_group = lax.broadcasted_iota(jnp.int32, (tiles_dev, group * ROWS), 0)
    lane_kind = lane_group & (ROWS - 1)
    west = lax.rem(lat + n_lat - 1, n_lat) * n_ray
    adjoint = smooth_adjoint
    row_total = jnp.zeros((1, 1), F32)
    for start in range(0, n_dev, group):
        letters = inbox[start : start + group]
        heads = jnp.sum(letters[:, 2, :], axis=0, keepdims=True)[:, : group * ROWS]
        row_total = row_total + jnp.sum(
            jnp.where(lane_kind == 2, heads, F32(0)), axis=1, keepdims=True
        )
        place = jnp.where(
            (lane_kind < 2) & (heads == (tile_group + 1).astype(F32)), F32(1), F32(0)
        )
        place = jnp.where(
            (tile_group == 0) & (lane_group == (west - start) * ROWS + 3), F32(-1), place
        )
        adjoint = adjoint + jnp.dot(
            place,
            letters.reshape(group * ROWS, block),
            precision=HIGHEST,
            preferred_element_type=F32,
        )

    beta = jnp.sqrt(row_total / rows_all + EPS)
    v_raw = ratio * adjoint / beta - beta * own
    square_row = jnp.sum(v_raw * v_raw, axis=0, keepdims=True)
    square[...] = square_row
    squares[lat] = square_row

    def send_square(step, carry):
        pltpu.make_async_remote_copy(
            src_ref=square,
            dst_ref=squares.at[lat],
            send_sem=send_sem.at[2],
            recv_sem=recv_sem.at[2],
            device_id=(lax.rem(lat + step, n_lat), ray),
            device_id_type=MESH,
        ).start()
        return carry

    lax.fori_loop(1, n_lat, send_square, 0)

    rhobar_old = recurrence[1]
    phibar_old = recurrence[2]
    rho = jnp.sqrt(rhobar_old * rhobar_old + beta * beta)
    cosine = rhobar_old / rho
    sine = beta / rho
    phi = cosine * phibar_old
    phibar = sine * phibar_old
    u_data_new[...] = data_raw[...] / beta
    for s in range(stencil):
        u_smooth_new[s] = smooth_raw[s] / beta
    x_new[...] = model_estimate[...] + phi / rho * direction[...]
    messages.wait_send()

    peers = pl.ds(0, n_lat - 1)
    sums = pltpu.make_async_remote_copy(
        src_ref=squares.at[peers],
        dst_ref=squares.at[peers],
        send_sem=send_sem.at[2],
        recv_sem=recv_sem.at[2],
        device_id=(lat, ray),
        device_id_type=MESH,
    )
    sums.wait_recv()
    model_square = jnp.sum(jnp.sum(squares[...], axis=0), axis=1, keepdims=True)
    alpha = jnp.sqrt(model_square / cell_count + EPS)
    theta = sine * alpha
    new = v_raw / alpha
    v_new[...] = new
    w_new[...] = new - theta / rho * direction[...]
    scalars[0] = alpha[0, 0]
    scalars[1] = beta[0, 0]
    scalars[2] = (-cosine * alpha)[0, 0]
    scalars[3] = phibar[0, 0]
    sums.wait_send()


def local(
    kernels,
    pattern,
    offsets,
    smooth_weight,
    u_data,
    u_smooth,
    right_vector,
    direction,
    model_estimate,
    recurrence,
):
    n_lat = lax.axis_size("lat")
    n_ray = lax.axis_size("ray")
    n_dev = n_lat * n_ray
    blocks_dev, kernel_count, block, _ = kernels.shape
    tiles_dev = right_vector.shape[0]
    stencil = offsets.shape[0]
    smem = pl.BlockSpec(memory_space=pltpu.SMEM)
    vmem = pl.BlockSpec(memory_space=pltpu.VMEM)
    like = lambda x: jax.ShapeDtypeStruct(x.shape, F32)
    return pl.pallas_call(
        functools.partial(kernel, n_lat, n_ray),
        out_shape=(
            like(u_data),
            like(u_smooth),
            like(right_vector),
            like(right_vector),
            like(right_vector),
            jax.ShapeDtypeStruct((4,), F32),
        ),
        in_specs=[smem] * 3 + [pl.BlockSpec(memory_space=pl.ANY)] + [vmem] * 6,
        out_specs=(vmem, vmem, vmem, vmem, vmem, smem),
        scratch_shapes=[
            pltpu.VMEM(kernels.shape, F32),
            pltpu.VMEM((n_lat * tiles_dev, block), F32),
            pltpu.VMEM((tiles_dev + 8, block), F32),
            pltpu.VMEM((stencil, tiles_dev + 8, block), F32),
            pltpu.VMEM((stencil, tiles_dev, block), F32),
            pltpu.VMEM((blocks_dev, block), F32),
            pltpu.VMEM((blocks_dev * kernel_count, block), F32),
            pltpu.VMEM((n_lat, ROWS, block), F32),
            pltpu.VMEM((n_dev, ROWS, block), F32),
            pltpu.VMEM((1, block), F32),
            pltpu.VMEM((n_lat, 1, block), F32),
            pltpu.SemaphoreType.DMA((2,)),
            pltpu.SemaphoreType.DMA((3,)),
            pltpu.SemaphoreType.DMA((3,)),
        ],
        compiler_params=pltpu.CompilerParams(collective_id=0, has_side_effects=True),
    )(
        pattern,
        offsets,
        recurrence,
        kernels,
        smooth_weight,
        u_data,
        u_smooth,
        right_vector,
        direction,
        model_estimate,
    )


def solution(mesh):
    return jax.shard_map(
        local,
        mesh=mesh,
        in_specs=(
            P(("lat", "ray"), None, None, None),
            P(("lat", "ray"), None),
            P(),
            P(None, "lat", None),
            P(("lat", "ray"), None),
            P(None, "lat", None),
            P("lat", None),
            P("lat", None),
            P("lat", None),
            P(),
        ),
        out_specs=(
            P(("lat", "ray"), None),
            P(None, "lat", None),
            P("lat", None),
            P("lat", None),
            P("lat", None),
            P(),
        ),
        check_vma=False,
    )
```

time: 160 us -> 33 us (0.21)
  blocking collectives: 78.6 us -> 0 us
  starting transfers between devices: 25 us -> 0 us
  Pallas kernels: 0 us -> 22.8 us
  between operations: 20.4 us -> 0.64 us
  other arithmetic: 8.21 us -> 0 us
  waiting for transfers between devices: 8.08 us -> 0 us
  local copies, waits for them, and re-layouts: 15.4 us -> 9.07 us
  matrix products: 3.18 us -> 0 us
    psum x3 -> x0, blocking collectives: 78.6 us -> none  [the longest x1 38.3 us: local(): model_sq = lax.psum(jnp.sum(v_raw * v_raw) / ray_count, ('lat', 'ray'))]
    pallas_call x0 -> x1, Pallas kernels: none -> 22.8 us  [local(): pl.pallas_call(functools.partial(kernel, n_lat, n_ray), out_shape=(like(u...]
    all_to_all x3 -> x0, starting transfers between devices: 16 us -> none  [the longest x1 6.88 us: local(): lax.all_to_all(tiles_out, 'lat', split_axis=0, concat_axis=0, tiled=True)]
    ppermute x2 -> x0, starting transfers between devices: 8.94 us -> none  [from_behind(): return lax.ppermute(value, axis, pairs)]
    unnamed x13 -> x7, local copies, waits for them, and re-layouts: 0.81 us -> 9.07 us
    scatter x2 -> x0, local copies, waits for them, and re-layouts: 5.81 us -> none  [the longest x1 3.79 us: local(): outgoing = jnp.zeros((lat_count, capacity, block), jnp.float32).at[owner_...]
    all_to_all x3 -> x0, waiting for transfers between devices: 4.08 us -> none  [the longest x1 4.07 us: local(): lax.all_to_all(outgoing, 'lat', split_axis=0, concat_axis=0, tiled=True)]
    ppermute x2 -> x0, waiting for transfers between devices: 4 us -> none  [from_behind(): return lax.ppermute(value, axis, pairs)]
  transfers between devices with their start and end apart: 5 -> 0, of which waited for: 2 -> 0; matrix products, arithmetic and copies ran while one was open for 9% -> 0% of each run, Pallas kernels for 0% -> 0%
where the time goes in v1:
time: 33 us; the launch traced here: 32.5 us
  Pallas kernels  22.8 us (69%)
  local copies, waits for them, and re-layouts  9.07 us (27%)
  between operations  0.64 us (2%)
    pallas_call x1, Pallas kernels, local(): pl.pallas_call(functools.partial(kernel, n_lat, n_ray), out_shape=(like(u...  22.8 us
    unnamed x7, local copies, waits for them, and re-layouts  9.07 us

profile of v1, /device:TPU:0, one launch (start us, length us, event | category | flops | bytes accessed | tf_op | source)
XLA Modules:
  0.0 32.5 jit_solution(10007111564266399464)
XLA Ops:
  0.6 1.3 %copy.16.pattern = s32[8,4]{1,0:T(8,128)} copy(s32[8,4]{0,1:T(4,128)} %param.11) | data formatting | bytes 256 | tf_op args[1]
  2.0 22.8 %shard_map.145 = (f32[8,128]{1,0:T(8,128)}, f32[4,16,128]{2,1,0:T(8,128)}, f32[16,128]{1,0:T(8,128)}, f32[16,128]{1,0:T(8,128)}, f32[16,128]{1,0:T(8,128)}, /*index=5*/f32[4]{0:T(128)}) custom-call(s32[8,4]{1,0:T(8,128)} %copy.16.pattern, s32[4]{0:T(128)} %offsets.1, f32[3]{0:T(128)} %recurrence.1, f32[8,4,128,128]{3,2,1,0:T(8,128)} %kernels_hbm.1, ...), custom_call_target="tpu_custom_call" | custom-call | tf_op jit(solution)/shard_map/pallas_call | solution.py:342
  24.8 1.3 %copy.23 = f32[8,128]{1,0:T(8,128)} copy(f32[8,128]{1,0:T(8,128)} %get-tuple-element.12) | data formatting | bytes 8192
  26.1 1.4 %copy.24 = f32[4,16,128]{2,1,0:T(8,128)} copy(f32[4,16,128]{2,1,0:T(8,128)} %get-tuple-element.13) | data formatting | bytes 65536
  27.5 1.3 %copy.25 = f32[16,128]{1,0:T(8,128)} copy(f32[16,128]{1,0:T(8,128)} %get-tuple-element.14) | data formatting | bytes 16384
  28.8 1.3 %copy.26 = f32[16,128]{1,0:T(8,128)} copy(f32[16,128]{1,0:T(8,128)} %get-tuple-element.15) | data formatting | bytes 16384
  30.1 1.3 %copy.27 = f32[16,128]{1,0:T(8,128)} copy(f32[16,128]{1,0:T(8,128)} %get-tuple-element.16) | data formatting | bytes 16384
  31.3 1.2 %copy.28 = f32[4]{0:T(128)} copy(f32[4]{0:T(128)} %get-tuple-element.17) | data formatting | bytes 32

commit v2 on v1

--- a/solution.py
+++ b/solution.py
@@ -12,29 +12,76 @@
 F32 = jnp.float32
 HIGHEST = lax.Precision.HIGHEST
 ROWS = 4
+VMEM_BYTES = 16 * 1024 * 1024
 GROUP = 32
+
+
+def plane_size(n_lat):
+    return 4 if n_lat % 4 == 0 else 1
+
+
+def partner(at, step, count):
+    if count & (count - 1):
+        return lax.rem(at + step, count)
+    result, bit = 0, 1
+    while bit < count:
+        result = result + bit * lax.rem(lax.div(at, bit) + step // bit, 2)
+        bit *= 2
+    return result
+
+
+def source(at, step, count):
+    return partner(at, count - step if count & (count - 1) else step, count)
+
+
+def each(count, body):
+    if count <= 64:
+        for step in range(count - 1, 0, -1):
+            body(step)
+    else:
+        lax.fori_loop(1, count, lambda step, carry: (body(count - step), carry)[1], 0)
+
+
+def deliver(*refs):
+    half = (len(refs) - 1) // 2
+    sems = refs[-1]
+    copies = [
+        pltpu.make_async_copy(refs[at], refs[half + at], sems.at[at]) for at in range(half)
+    ]
+    for copy in copies:
+        copy.start()
+    for copy in copies:
+        copy.wait()
 
 
 def kernel(
     n_lat,
     n_ray,
-    pattern,
-    offsets,
-    recurrence,
-    kernels_hbm,
-    smooth_weight,
-    u_data,
-    u_smooth,
-    right_vector,
-    direction,
-    model_estimate,
+    pattern_in,
+    offsets_in,
+    recurrence_in,
+    kernels_in,
+    smooth_weight_in,
+    u_data_in,
+    u_smooth_in,
+    right_vector_in,
+    direction_in,
+    model_estimate_in,
     u_data_new,
     u_smooth_new,
     v_new,
     w_new,
     x_new,
     scalars,
+    pattern,
+    offsets,
+    recurrence,
     held,
+    smooth_weight,
+    u_data,
+    u_smooth,
+    direction,
+    model_estimate,
     full,
     window,
     padded,
@@ -46,6 +93,7 @@
     square,
     squares,
     local_sem,
+    band_sem,
     send_sem,
     recv_sem,
 ):
@@ -54,47 +102,78 @@
     n_dev = n_lat * n_ray
     me = lat * n_ray + ray
     blocks_dev, kernel_count, block, _ = held.shape
-    tiles_dev = right_vector.shape[0]
+    tiles_dev = right_vector_in.shape[0]
     stencil = smooth_weight.shape[0]
     slots = blocks_dev * kernel_count
     cell_count = n_lat * tiles_dev * block
     rows_all = n_dev * blocks_dev * block + stencil * cell_count
     ratio = cell_count / rows_all
 
-    fetch = pltpu.make_async_copy(kernels_hbm, held, local_sem.at[0])
-    fetch.start()
-    own_band = pltpu.make_async_copy(
-        right_vector, full.at[pl.ds(lat * tiles_dev, tiles_dev)], local_sem.at[1]
-    )
+    n_inner = plane_size(n_lat)
+    n_outer = n_lat // n_inner
+    outer, inner = lax.div(lat, n_inner), lax.rem(lat, n_inner)
+
+    barrier = pltpu.get_barrier_semaphore()
+
+    def greet(device):
+        pl.semaphore_signal(barrier, inc=1, device_id=device, device_id_type=MESH)
+
+    for step in range(n_outer - 1, 0, -1):
+        greet((partner(outer, step, n_outer) * n_inner + inner, ray))
+    for step in range(1, n_inner):
+        greet((outer * n_inner + partner(inner, step, n_inner), ray))
+    for step in range(1, n_ray):
+        greet((lat, partner(ray, step, n_ray)))
+
+    def band_of(index):
+        return full.at[pl.ds(pl.multiple_of(index * tiles_dev, tiles_dev), tiles_dev)]
+
+    own_band = pltpu.make_async_copy(right_vector_in, band_of(lat), local_sem.at[0])
     own_band.start()
-
-    barrier = pltpu.get_barrier_semaphore()
-
-    def greet(step, carry):
-        other = lax.rem(me + step, n_dev)
-        pl.semaphore_signal(
-            barrier,
-            inc=1,
-            device_id=(lax.div(other, n_ray), lax.rem(other, n_ray)),
+    fetches = [
+        pltpu.make_async_copy(source, target, local_sem.at[1 + at])
+        for at, (source, target) in enumerate(
+            (
+                (pattern_in, pattern),
+                (offsets_in, offsets),
+                (recurrence_in, recurrence),
+                (smooth_weight_in, smooth_weight),
+                (u_data_in, u_data),
+                (u_smooth_in, u_smooth),
+                (direction_in, direction),
+                (model_estimate_in, model_estimate),
+                (kernels_in, held),
+            )
+        )
+    ]
+    for fetch in fetches:
+        fetch.start()
+    own_band.wait()
+    pl.semaphore_wait(barrier, n_outer + n_inner + n_ray - 3)
+
+    def copy_band(index, slot, device):
+        return pltpu.make_async_remote_copy(
+            src_ref=band_of(index),
+            dst_ref=band_of(index),
+            send_sem=send_sem.at[0],
+            recv_sem=band_sem.at[slot],
+            device_id=device,
             device_id_type=MESH,
         )
-        return carry
-
-    lax.fori_loop(1, n_dev, greet, 0)
-    pl.semaphore_wait(barrier, n_dev - 1)
-
-    def send_band(step, carry):
-        pltpu.make_async_remote_copy(
-            src_ref=right_vector,
-            dst_ref=full.at[pl.ds(lat * tiles_dev, tiles_dev)],
-            send_sem=send_sem.at[0],
-            recv_sem=recv_sem.at[0],
-            device_id=(lax.rem(lat + step, n_lat), ray),
-            device_id_type=MESH,
+
+    def forward(index, slot):
+        for step in range(n_inner - 1, 0, -1):
+            copy_band(
+                index, slot * n_inner + step, (outer * n_inner + partner(inner, step, n_inner), ray)
+            ).start()
+
+    for step in range(n_outer - 1, 0, -1):
+        copy_band(
+            lat, step * n_inner, (partner(outer, step, n_outer) * n_inner + inner, ray)
         ).start()
-        return carry
-
-    lax.fori_loop(1, n_lat, send_band, 0)
+    forward(lat, 0)
+    for fetch in fetches[:3]:
+        fetch.wait()
 
     alpha_old = recurrence[0]
     lane_slot = lax.broadcasted_iota(jnp.int32, (1, slots), 1)
@@ -102,7 +181,7 @@
     for b in range(blocks_dev):
         for k in range(kernel_count):
             tile_row = jnp.where(
-                lane_slot == b * kernel_count + k, pattern[b, k].astype(F32), tile_row
+                lane_slot == b * kernel_count + k, pattern[k, b].astype(F32), tile_row
             )
     shape = (n_lat * ROWS, slots)
     message_row = lax.broadcasted_iota(jnp.int32, shape, 0)
@@ -130,18 +209,18 @@
     header = jnp.where(kind_wide == 2, header, F32(0))
     is_total = (kind_wide == 2) & (lane_wide == mark + 2)
 
-    fetch.wait()
-    own_band.wait()
-    rest = pl.ds(0, (n_lat - 1) * tiles_dev)
-    bands = pltpu.make_async_remote_copy(
-        src_ref=full.at[rest],
-        dst_ref=full.at[rest],
-        send_sem=send_sem.at[0],
-        recv_sem=recv_sem.at[0],
-        device_id=(lat, ray),
-        device_id_type=MESH,
-    )
-    bands.wait_recv()
+    for step in range(1, n_outer):
+        index = source(outer, step, n_outer) * n_inner + inner
+        copy_band(index, step * n_inner, (lat, ray)).wait_recv()
+        forward(index, step)
+    for fetch in fetches[3:]:
+        fetch.wait()
+    for step in range(n_outer):
+        column = source(outer, step, n_outer) * n_inner
+        for turn in range(1, n_inner):
+            copy_band(
+                column + source(inner, turn, n_inner), step * n_inner + turn, (lat, ray)
+            ).wait_recv()
 
     diagonal = lax.broadcasted_iota(jnp.int32, (block, block), 0) == lax.broadcasted_iota(
         jnp.int32, (block, block), 1
@@ -149,7 +228,7 @@
     for b in range(blocks_dev):
         total = jnp.where(diagonal, -alpha_old * u_data[b : b + 1, :], F32(0))
         for k in range(kernel_count):
-            total = total + held[b, k] * full[pl.ds(pattern[b, k], 1), :]
+            total = total + held[b, k] * full[pl.ds(pattern[k, b], 1), :]
         column = jnp.sum(total, axis=1, keepdims=True)
         data_raw[b : b + 1, :] = jnp.sum(
             jnp.where(diagonal, column, F32(0)), axis=0, keepdims=True
@@ -159,7 +238,7 @@
                 held[b, k] * column, axis=0, keepdims=True
             )
 
-    own = right_vector[...]
+    own = full[pl.ds(pl.multiple_of(lat * tiles_dev, tiles_dev), tiles_dev), :]
     lane = lax.broadcasted_iota(jnp.int32, (1, block), 1)
     window[0:tiles_dev, :] = own
     window[tiles_dev : tiles_dev + 1, :] = full[
@@ -197,19 +276,19 @@
     for band in range(n_lat):
         message[band] = outgoing[band * ROWS : (band + 1) * ROWS, :]
 
-    def send_message(step, carry):
-        other = lax.rem(me + step, n_dev)
+    def send_message(step):
+        row = partner(lat, step // n_ray, n_lat)
+        core = partner(ray, step % n_ray, n_ray)
         pltpu.make_async_remote_copy(
-            src_ref=message.at[lax.div(other, n_ray)],
+            src_ref=message.at[row],
             dst_ref=inbox.at[me],
             send_sem=send_sem.at[1],
-            recv_sem=recv_sem.at[1],
-            device_id=(lax.div(other, n_ray), lax.rem(other, n_ray)),
+            recv_sem=recv_sem.at[0],
+            device_id=(row, core),
             device_id_type=MESH,
         ).start()
-        return carry
-
-    lax.fori_loop(1, n_dev, send_message, 0)
+
+    each(n_dev, send_message)
     inbox[me] = message[lat]
 
     smooth_adjoint = jnp.zeros((tiles_dev, block), F32)
@@ -225,13 +304,14 @@
         )
         smooth_adjoint = smooth_adjoint + (weighted - behind)
 
-    bands.wait_send()
+    for _ in range(n_outer - 1 + n_outer * (n_inner - 1)):
+        copy_band(lat, 0, (lat, ray)).wait_send()
     others = pl.ds(0, n_dev - 1)
     messages = pltpu.make_async_remote_copy(
         src_ref=inbox.at[others],
         dst_ref=inbox.at[others],
         send_sem=send_sem.at[1],
-        recv_sem=recv_sem.at[1],
+        recv_sem=recv_sem.at[0],
         device_id=(lat, ray),
         device_id_type=MESH,
     )
@@ -269,18 +349,17 @@
     square[...] = square_row
     squares[lat] = square_row
 
-    def send_square(step, carry):
+    def send_square(step):
         pltpu.make_async_remote_copy(
             src_ref=square,
             dst_ref=squares.at[lat],
             send_sem=send_sem.at[2],
-            recv_sem=recv_sem.at[2],
-            device_id=(lax.rem(lat + step, n_lat), ray),
+            recv_sem=recv_sem.at[1],
+            device_id=(partner(lat, step, n_lat), ray),
             device_id_type=MESH,
         ).start()
-        return carry
-
-    lax.fori_loop(1, n_lat, send_square, 0)
+
+    each(n_lat, send_square)
 
     rhobar_old = recurrence[1]
     phibar_old = recurrence[2]
@@ -300,7 +379,7 @@
         src_ref=squares.at[peers],
         dst_ref=squares.at[peers],
         send_sem=send_sem.at[2],
-        recv_sem=recv_sem.at[2],
+        recv_sem=recv_sem.at[1],
         device_id=(lat, ray),
         device_id_type=MESH,
     )
@@ -339,7 +418,8 @@
     smem = pl.BlockSpec(memory_space=pltpu.SMEM)
     vmem = pl.BlockSpec(memory_space=pltpu.VMEM)
     like = lambda x: jax.ShapeDtypeStruct(x.shape, F32)
-    return pl.pallas_call(
+    n_inner = plane_size(n_lat)
+    results = pl.pallas_call(
         functools.partial(kernel, n_lat, n_ray),
         out_shape=(
             like(u_data),
@@ -349,10 +429,18 @@
             like(right_vector),
             jax.ShapeDtypeStruct((4,), F32),
         ),
-        in_specs=[smem] * 3 + [pl.BlockSpec(memory_space=pl.ANY)] + [vmem] * 6,
+        in_specs=[pl.BlockSpec(memory_space=pltpu.HBM)] * 10,
         out_specs=(vmem, vmem, vmem, vmem, vmem, smem),
         scratch_shapes=[
+            pltpu.SMEM((kernel_count, blocks_dev), jnp.int32),
+            pltpu.SMEM(offsets.shape, jnp.int32),
+            pltpu.SMEM(recurrence.shape, F32),
             pltpu.VMEM(kernels.shape, F32),
+            pltpu.VMEM(smooth_weight.shape, F32),
+            pltpu.VMEM(u_data.shape, F32),
+            pltpu.VMEM(u_smooth.shape, F32),
+            pltpu.VMEM(direction.shape, F32),
+            pltpu.VMEM(model_estimate.shape, F32),
             pltpu.VMEM((n_lat * tiles_dev, block), F32),
             pltpu.VMEM((tiles_dev + 8, block), F32),
             pltpu.VMEM((stencil, tiles_dev + 8, block), F32),
@@ -363,23 +451,39 @@
             pltpu.VMEM((n_dev, ROWS, block), F32),
             pltpu.VMEM((1, block), F32),
             pltpu.VMEM((n_lat, 1, block), F32),
+            pltpu.SemaphoreType.DMA((10,)),
+            pltpu.SemaphoreType.DMA((n_lat,)),
+            pltpu.SemaphoreType.DMA((3,)),
             pltpu.SemaphoreType.DMA((2,)),
-            pltpu.SemaphoreType.DMA((3,)),
-            pltpu.SemaphoreType.DMA((3,)),
         ],
-        compiler_params=pltpu.CompilerParams(collective_id=0, has_side_effects=True),
+        compiler_params=pltpu.CompilerParams(
+            collective_id=0, has_side_effects=True, vmem_limit_bytes=VMEM_BYTES
+        ),
     )(
-        pattern,
-        offsets,
-        recurrence,
-        kernels,
-        smooth_weight,
-        u_data,
-        u_smooth,
-        right_vector,
-        direction,
-        model_estimate,
-    )
+        *(
+            pltpu.with_memory_space_constraint(x, pltpu.HBM)
+            for x in (
+                pattern.T,
+                offsets,
+                recurrence,
+                kernels,
+                smooth_weight,
+                u_data,
+                u_smooth,
+                right_vector,
+                direction,
+                model_estimate,
+            )
+        )
+    )
+    return pl.pallas_call(
+        deliver,
+        out_shape=tuple(like(x) for x in results),
+        in_specs=[vmem] * 5 + [smem],
+        out_specs=(pl.BlockSpec(memory_space=pltpu.HBM),) * 6,
+        scratch_shapes=[pltpu.SemaphoreType.DMA((6,))],
+        compiler_params=pltpu.CompilerParams(vmem_limit_bytes=VMEM_BYTES),
+    )(*results)
 
 
 def solution(mesh):

time: 33 us -> 24.9 us (0.75)
  local copies, waits for them, and re-layouts: 9.07 us -> 0 us
  Pallas kernels: 22.8 us -> 24.1 us
    unnamed x7 -> x0, local copies, waits for them, and re-layouts: 9.07 us -> none
    pallas_call x0 -> x1, Pallas kernels: none -> 1.23 us  [local(): pl.pallas_call(deliver, out_shape=tuple((like(x) for x in results)), in_s...]
where the time goes in v2:
time: 24.9 us; the launch traced here: 24.7 us
  Pallas kernels  24.1 us (97%)
  between operations  0.64 us (3%)
    pallas_call x1, Pallas kernels, local(): pl.pallas_call(functools.partial(kernel, n_lat, n_ray), out_shape=(like(u...  22.8 us
    pallas_call x1, Pallas kernels, local(): pl.pallas_call(deliver, out_shape=tuple((like(x) for x in results)), in_s...  1.23 us

profile of v2, /device:TPU:0, one launch (start us, length us, event | category | flops | bytes accessed | tf_op | source)
XLA Modules:
  0.0 24.7 jit_solution(180481219488769919)
XLA Ops:
  0.6 22.8 %shard_map.145 = (f32[8,128]{1,0:T(8,128)S(1)}, f32[4,16,128]{2,1,0:T(8,128)S(1)}, f32[16,128]{1,0:T(8,128)S(1)}, f32[16,128]{1,0:T(8,128)S(1)}, f32[16,128]{1,0:T(8,128)S(1)}, /*index=5*/f32[4]{0:T(128)S(1)}) custom-call(s32[4,8]{1,0:T(4,128)} %bitcast.1, s32[4]{0:T(128)} %offsets_in.1, f32[3]{0:T(128)} %recurrence_in.1, f32[8,4,128,128]{3,2,1,0:T(8,128)} %kernels_in.1, ...), custom_call_target="tpu_custom_call" | custom-call | tf_op jit(solution)/shard_map/pallas_call | solution.py:422
  23.5 1.2 %shard_map.146 = (f32[8,128]{1,0:T(8,128)}, f32[4,16,128]{2,1,0:T(8,128)}, f32[16,128]{1,0:T(8,128)}, f32[16,128]{1,0:T(8,128)}, f32[16,128]{1,0:T(8,128)}, /*index=5*/f32[4]{0:T(128)}) custom-call(f32[8,128]{1,0:T(8,128)S(1)} %get-tuple-element.12.refs_0_, f32[4,16,128]{2,1,0:T(8,128)S(1)} %get-tuple-element.13.refs_1_, ...), custom_call_target="tpu_custom_call" | custom-call | tf_op jit(solution)/shard_map/pallas_call | solution.py:479

commit v3 on v2

--- a/solution.py
+++ b/solution.py
@@ -10,10 +10,20 @@
 EPS = 1e-06
 MESH = pl.DeviceIdType.MESH
 F32 = jnp.float32
-HIGHEST = lax.Precision.HIGHEST
 ROWS = 4
 VMEM_BYTES = 16 * 1024 * 1024
 GROUP = 32
+
+
+def select(place, values):
+    place = place.astype(jnp.bfloat16)
+    total, rest = None, values
+    for _ in range(3):
+        part = rest.astype(jnp.bfloat16)
+        rest = rest - part.astype(F32)
+        term = jnp.dot(place, part, preferred_element_type=F32)
+        total = term if total is None else total + term
+    return total
 
 
 def plane_size(n_lat):
@@ -118,12 +128,10 @@
     def greet(device):
         pl.semaphore_signal(barrier, inc=1, device_id=device, device_id_type=MESH)
 
-    for step in range(n_outer - 1, 0, -1):
-        greet((partner(outer, step, n_outer) * n_inner + inner, ray))
-    for step in range(1, n_inner):
-        greet((outer * n_inner + partner(inner, step, n_inner), ray))
-    for step in range(1, n_ray):
-        greet((lat, partner(ray, step, n_ray)))
+    def greet_all(step):
+        greet((partner(lat, step // n_ray, n_lat), partner(ray, step % n_ray, n_ray)))
+
+    each(n_dev, greet_all)
 
     def band_of(index):
         return full.at[pl.ds(pl.multiple_of(index * tiles_dev, tiles_dev), tiles_dev)]
@@ -149,7 +157,7 @@
     for fetch in fetches:
         fetch.start()
     own_band.wait()
-    pl.semaphore_wait(barrier, n_outer + n_inner + n_ray - 3)
+    pl.semaphore_wait(barrier, n_dev - 1)
 
     def copy_band(index, slot, device):
         return pltpu.make_async_remote_copy(
@@ -167,11 +175,8 @@
                 index, slot * n_inner + step, (outer * n_inner + partner(inner, step, n_inner), ray)
             ).start()
 
-    for step in range(n_outer - 1, 0, -1):
-        copy_band(
-            lat, step * n_inner, (partner(outer, step, n_outer) * n_inner + inner, ray)
-        ).start()
-    forward(lat, 0)
+    for step in range(n_lat - 1, 0, -1):
+        copy_band(lat, step, (partner(lat, step, n_lat), ray)).start()
     for fetch in fetches[:3]:
         fetch.wait()
 
@@ -209,18 +214,10 @@
     header = jnp.where(kind_wide == 2, header, F32(0))
     is_total = (kind_wide == 2) & (lane_wide == mark + 2)
 
-    for step in range(1, n_outer):
-        index = source(outer, step, n_outer) * n_inner + inner
-        copy_band(index, step * n_inner, (lat, ray)).wait_recv()
-        forward(index, step)
     for fetch in fetches[3:]:
         fetch.wait()
-    for step in range(n_outer):
-        column = source(outer, step, n_outer) * n_inner
-        for turn in range(1, n_inner):
-            copy_band(
-                column + source(inner, turn, n_inner), step * n_inner + turn, (lat, ray)
-            ).wait_recv()
+    for step in range(1, n_lat):
+        copy_band(lat, step, (lat, ray)).wait_recv()
 
     diagonal = lax.broadcasted_iota(jnp.int32, (block, block), 0) == lax.broadcasted_iota(
         jnp.int32, (block, block), 1
@@ -266,7 +263,7 @@
     )
     local_total = jnp.sum(row_sum, axis=1, keepdims=True)
 
-    picked = jnp.dot(selector, contrib[...], precision=HIGHEST, preferred_element_type=F32)
+    picked = select(selector, contrib[...])
     outgoing = (
         picked
         + header
@@ -304,7 +301,7 @@
         )
         smooth_adjoint = smooth_adjoint + (weighted - behind)
 
-    for _ in range(n_outer - 1 + n_outer * (n_inner - 1)):
+    for _ in range(n_lat - 1):
         copy_band(lat, 0, (lat, ray)).wait_send()
     others = pl.ds(0, n_dev - 1)
     messages = pltpu.make_async_remote_copy(
@@ -336,15 +333,10 @@
         place = jnp.where(
             (tile_group == 0) & (lane_group == (west - start) * ROWS + 3), F32(-1), place
         )
-        adjoint = adjoint + jnp.dot(
-            place,
-            letters.reshape(group * ROWS, block),
-            precision=HIGHEST,
-            preferred_element_type=F32,
-        )
+        adjoint = adjoint + select(place, letters.reshape(group * ROWS, block))
 
     beta = jnp.sqrt(row_total / rows_all + EPS)
-    v_raw = ratio * adjoint / beta - beta * own
+    v_raw = adjoint * (ratio / beta) - beta * own
     square_row = jnp.sum(v_raw * v_raw, axis=0, keepdims=True)
     square[...] = square_row
     squares[lat] = square_row
@@ -372,6 +364,8 @@
     for s in range(stencil):
         u_smooth_new[s] = smooth_raw[s] / beta
     x_new[...] = model_estimate[...] + phi / rho * direction[...]
+    scalars[1] = beta[0, 0]
+    scalars[3] = phibar[0, 0]
     messages.wait_send()
 
     peers = pl.ds(0, n_lat - 1)
@@ -391,9 +385,7 @@
     v_new[...] = new
     w_new[...] = new - theta / rho * direction[...]
     scalars[0] = alpha[0, 0]
-    scalars[1] = beta[0, 0]
     scalars[2] = (-cosine * alpha)[0, 0]
-    scalars[3] = phibar[0, 0]
     sums.wait_send()
 
 

time: 24.9 us -> 24.1 us (0.968)
  Pallas kernels: 24.1 us -> 23.2 us
    pallas_call x1, Pallas kernels: 22.8 us -> 22 us  [local(): pl.pallas_call(functools.partial(kernel, n_lat, n_ray), out_shape=(like(u...]
where the time goes in v3:
time: 24.1 us; the launch traced here: 23.9 us
  Pallas kernels  23.2 us (96%)
  between operations  0.64 us (3%)
    pallas_call x1, Pallas kernels, local(): pl.pallas_call(functools.partial(kernel, n_lat, n_ray), out_shape=(like(u...  22 us
    pallas_call x1, Pallas kernels, local(): pl.pallas_call(deliver, out_shape=tuple((like(x) for x in results)), in_s...  1.23 us

profile of v3, /device:TPU:0, one launch (start us, length us, event | category | flops | bytes accessed | tf_op | source)
XLA Modules:
  0.0 23.9 jit_solution(6316304035818393605)
XLA Ops:
  0.6 22.0 %shard_map.145 = (f32[8,128]{1,0:T(8,128)S(1)}, f32[4,16,128]{2,1,0:T(8,128)S(1)}, f32[16,128]{1,0:T(8,128)S(1)}, f32[16,128]{1,0:T(8,128)S(1)}, f32[16,128]{1,0:T(8,128)S(1)}, /*index=5*/f32[4]{0:T(128)S(1)}) custom-call(s32[4,8]{1,0:T(4,128)} %bitcast.1, s32[4]{0:T(128)} %offsets_in.1, f32[3]{0:T(128)} %recurrence_in.1, f32[8,4,128,128]{3,2,1,0:T(8,128)} %kernels_in.1, ...), custom_call_target="tpu_custom_call" | custom-call | tf_op jit(solution)/shard_map/pallas_call | solution.py:414
  22.6 1.2 %shard_map.146 = (f32[8,128]{1,0:T(8,128)}, f32[4,16,128]{2,1,0:T(8,128)}, f32[16,128]{1,0:T(8,128)}, f32[16,128]{1,0:T(8,128)}, f32[16,128]{1,0:T(8,128)}, /*index=5*/f32[4]{0:T(128)}) custom-call(f32[8,128]{1,0:T(8,128)S(1)} %get-tuple-element.12.refs_0_, f32[4,16,128]{2,1,0:T(8,128)S(1)} %get-tuple-element.13.refs_1_, ...), custom_call_target="tpu_custom_call" | custom-call | tf_op jit(solution)/shard_map/pallas_call | solution.py:471

commit v4 on v3

--- a/solution.py
+++ b/solution.py
@@ -159,24 +159,26 @@
     own_band.wait()
     pl.semaphore_wait(barrier, n_dev - 1)
 
-    def copy_band(index, slot, device):
+    parts = n_ray if n_ray == 2 and tiles_dev % (8 * n_ray) == 0 else 1
+    part_rows = tiles_dev // parts
+    part = ray if parts > 1 else 0
+    other_ray = partner(ray, 1, n_ray)
+
+    def copy_band(index, which, slot, device):
+        rows = pl.ds(
+            pl.multiple_of(index * tiles_dev + which * part_rows, part_rows), part_rows
+        )
         return pltpu.make_async_remote_copy(
-            src_ref=band_of(index),
-            dst_ref=band_of(index),
+            src_ref=full.at[rows],
+            dst_ref=full.at[rows],
             send_sem=send_sem.at[0],
             recv_sem=band_sem.at[slot],
             device_id=device,
             device_id_type=MESH,
         )
 
-    def forward(index, slot):
-        for step in range(n_inner - 1, 0, -1):
-            copy_band(
-                index, slot * n_inner + step, (outer * n_inner + partner(inner, step, n_inner), ray)
-            ).start()
-
     for step in range(n_lat - 1, 0, -1):
-        copy_band(lat, step, (partner(lat, step, n_lat), ray)).start()
+        copy_band(lat, part, step, (partner(lat, step, n_lat), ray)).start()
     for fetch in fetches[:3]:
         fetch.wait()
 
@@ -214,10 +216,18 @@
     header = jnp.where(kind_wide == 2, header, F32(0))
     is_total = (kind_wide == 2) & (lane_wide == mark + 2)
 
+    for step in range(1, n_lat):
+        index = source(lat, step, n_lat)
+        copy_band(index, part, step, (lat, ray)).wait_recv()
+        if parts > 1:
+            copy_band(index, part, n_lat + step, (lat, other_ray)).start()
     for fetch in fetches[3:]:
         fetch.wait()
-    for step in range(1, n_lat):
-        copy_band(lat, step, (lat, ray)).wait_recv()
+    if parts > 1:
+        for step in range(1, n_lat):
+            copy_band(
+                source(lat, step, n_lat), other_ray, n_lat + step, (lat, ray)
+            ).wait_recv()
 
     diagonal = lax.broadcasted_iota(jnp.int32, (block, block), 0) == lax.broadcasted_iota(
         jnp.int32, (block, block), 1
@@ -301,8 +311,8 @@
         )
         smooth_adjoint = smooth_adjoint + (weighted - behind)
 
-    for _ in range(n_lat - 1):
-        copy_band(lat, 0, (lat, ray)).wait_send()
+    for _ in range((n_lat - 1) * parts):
+        copy_band(lat, part, 0, (lat, ray)).wait_send()
     others = pl.ds(0, n_dev - 1)
     messages = pltpu.make_async_remote_copy(
         src_ref=inbox.at[others],
@@ -444,7 +454,7 @@
             pltpu.VMEM((1, block), F32),
             pltpu.VMEM((n_lat, 1, block), F32),
             pltpu.SemaphoreType.DMA((10,)),
-            pltpu.SemaphoreType.DMA((n_lat,)),
+            pltpu.SemaphoreType.DMA((2 * n_lat,)),
             pltpu.SemaphoreType.DMA((3,)),
             pltpu.SemaphoreType.DMA((2,)),
         ],

time: 24.1 us -> 23.8 us (0.988)
  Pallas kernels: 23.2 us -> 22.9 us
    pallas_call x1, Pallas kernels: 22 us -> 21.7 us  [local(): pl.pallas_call(functools.partial(kernel, n_lat, n_ray), out_shape=(like(u...]
where the time goes in v4:
time: 23.8 us; the launch traced here: 23.5 us
  Pallas kernels  22.9 us (96%)
  between operations  0.64 us (3%)
    pallas_call x1, Pallas kernels, local(): pl.pallas_call(functools.partial(kernel, n_lat, n_ray), out_shape=(like(u...  21.7 us
    pallas_call x1, Pallas kernels, local(): pl.pallas_call(deliver, out_shape=tuple((like(x) for x in results)), in_s...  1.23 us

profile of v4, /device:TPU:0, one launch (start us, length us, event | category | flops | bytes accessed | tf_op | source)
XLA Modules:
  0.0 23.5 jit_solution(18206646614046977222)
XLA Ops:
  0.6 21.7 %shard_map.145 = (f32[8,128]{1,0:T(8,128)S(1)}, f32[4,16,128]{2,1,0:T(8,128)S(1)}, f32[16,128]{1,0:T(8,128)S(1)}, f32[16,128]{1,0:T(8,128)S(1)}, f32[16,128]{1,0:T(8,128)S(1)}, /*index=5*/f32[4]{0:T(128)S(1)}) custom-call(s32[4,8]{1,0:T(4,128)} %bitcast.1, s32[4]{0:T(128)} %offsets_in.1, f32[3]{0:T(128)} %recurrence_in.1, f32[8,4,128,128]{3,2,1,0:T(8,128)} %kernels_in.1, ...), custom_call_target="tpu_custom_call" | custom-call | tf_op jit(solution)/shard_map/pallas_call | solution.py:424
  22.3 1.2 %shard_map.146 = (f32[8,128]{1,0:T(8,128)}, f32[4,16,128]{2,1,0:T(8,128)}, f32[16,128]{1,0:T(8,128)}, f32[16,128]{1,0:T(8,128)}, f32[16,128]{1,0:T(8,128)}, /*index=5*/f32[4]{0:T(128)}) custom-call(f32[8,128]{1,0:T(8,128)S(1)} %get-tuple-element.12.refs_0_, f32[4,16,128]{2,1,0:T(8,128)S(1)} %get-tuple-element.13.refs_1_, ...), custom_call_target="tpu_custom_call" | custom-call | tf_op jit(solution)/shard_map/pallas_call | solution.py:481

commit v5 on v4

--- a/solution.py
+++ b/solution.py
@@ -349,12 +349,12 @@
     v_raw = adjoint * (ratio / beta) - beta * own
     square_row = jnp.sum(v_raw * v_raw, axis=0, keepdims=True)
     square[...] = square_row
-    squares[lat] = square_row
+    squares[pl.ds(lat, 1), :] = square_row
 
     def send_square(step):
         pltpu.make_async_remote_copy(
             src_ref=square,
-            dst_ref=squares.at[lat],
+            dst_ref=squares.at[pl.ds(lat, 1)],
             send_sem=send_sem.at[2],
             recv_sem=recv_sem.at[1],
             device_id=(partner(lat, step, n_lat), ray),
@@ -374,6 +374,7 @@
     for s in range(stencil):
         u_smooth_new[s] = smooth_raw[s] / beta
     x_new[...] = model_estimate[...] + phi / rho * direction[...]
+    turned_direction = sine / rho * direction[...]
     scalars[1] = beta[0, 0]
     scalars[3] = phibar[0, 0]
     messages.wait_send()
@@ -388,12 +389,11 @@
         device_id_type=MESH,
     )
     sums.wait_recv()
-    model_square = jnp.sum(jnp.sum(squares[...], axis=0), axis=1, keepdims=True)
+    model_square = jnp.sum(jnp.sum(squares[...], axis=0, keepdims=True), axis=1, keepdims=True)
     alpha = jnp.sqrt(model_square / cell_count + EPS)
-    theta = sine * alpha
-    new = v_raw / alpha
+    new = v_raw * (1.0 / alpha)
     v_new[...] = new
-    w_new[...] = new - theta / rho * direction[...]
+    w_new[...] = new - alpha * turned_direction
     scalars[0] = alpha[0, 0]
     scalars[2] = (-cosine * alpha)[0, 0]
     sums.wait_send()
@@ -452,7 +452,7 @@
             pltpu.VMEM((n_lat, ROWS, block), F32),
             pltpu.VMEM((n_dev, ROWS, block), F32),
             pltpu.VMEM((1, block), F32),
-            pltpu.VMEM((n_lat, 1, block), F32),
+            pltpu.VMEM((n_lat, block), F32),
             pltpu.SemaphoreType.DMA((10,)),
             pltpu.SemaphoreType.DMA((2 * n_lat,)),
             pltpu.SemaphoreType.DMA((3,)),

time: 23.8 us -> 23.8 us (level)
  no operation moved by 1% of the time
where the time goes in v5:
time: 23.8 us; the launch traced here: 23.5 us
  Pallas kernels  22.9 us (96%)
  between operations  0.64 us (3%)
    pallas_call x1, Pallas kernels, local(): pl.pallas_call(functools.partial(kernel, n_lat, n_ray), out_shape=(like(u...  21.7 us
    pallas_call x1, Pallas kernels, local(): pl.pallas_call(deliver, out_shape=tuple((like(x) for x in results)), in_s...  1.23 us

profile of v5, /device:TPU:0, one launch (start us, length us, event | category | flops | bytes accessed | tf_op | source)
XLA Modules:
  0.0 23.5 jit_solution(4415652281738618965)
XLA Ops:
  0.6 21.7 %shard_map.145 = (f32[8,128]{1,0:T(8,128)S(1)}, f32[4,16,128]{2,1,0:T(8,128)S(1)}, f32[16,128]{1,0:T(8,128)S(1)}, f32[16,128]{1,0:T(8,128)S(1)}, f32[16,128]{1,0:T(8,128)S(1)}, /*index=5*/f32[4]{0:T(128)S(1)}) custom-call(s32[4,8]{1,0:T(4,128)} %bitcast.1, s32[4]{0:T(128)} %offsets_in.1, f32[3]{0:T(128)} %recurrence_in.1, f32[8,4,128,128]{3,2,1,0:T(8,128)} %kernels_in.1, ...), custom_call_target="tpu_custom_call" | custom-call | tf_op jit(solution)/shard_map/pallas_call | solution.py:424
  22.3 1.2 %shard_map.146 = (f32[8,128]{1,0:T(8,128)}, f32[4,16,128]{2,1,0:T(8,128)}, f32[16,128]{1,0:T(8,128)}, f32[16,128]{1,0:T(8,128)}, f32[16,128]{1,0:T(8,128)}, /*index=5*/f32[4]{0:T(128)}) custom-call(f32[8,128]{1,0:T(8,128)S(1)} %get-tuple-element.12.refs_0_, f32[4,16,128]{2,1,0:T(8,128)S(1)} %get-tuple-element.13.refs_1_, ...), custom_call_target="tpu_custom_call" | custom-call | tf_op jit(solution)/shard_map/pallas_call | solution.py:481
